TPU v7x, 256 devices: a whole 4x4x8 slice. The times are simulated.
256 devices in a mesh: replica: 4 (over z_hi, core), fsdp: 64 (over z_lo, x, y).
Axes of the slice: x: 4, y: 4, z: 8 (z_hi: 2, z_lo: 4; z = z_hi * 4 + z_lo), core: 2. Of those that a mesh axis runs over, the one named last changes fastest.
Arguments:
- tokens: bfloat16 [65536, 2048], P(('replica', 'fsdp')), may hold values from -6 to 6
- inner_q: bfloat16 [4, 2048, 2048], P('replica', 'fsdp')
- inner_k: bfloat16 [4, 2048, 512], P('replica', 'fsdp')
- inner_v: bfloat16 [4, 2048, 512], P('replica', 'fsdp')
- outer_q: float32 [2048, 2048], P('fsdp')
- outer_k: float32 [2048, 512], P('fsdp')
- outer_v: float32 [2048, 512], P('fsdp')
- moment_q: float32 [2048, 2048], P('fsdp', 'replica'), may hold values from -0.09375 to 0.09375
- moment_k: float32 [2048, 512], P('fsdp', 'replica'), may hold values from -0.09375 to 0.09375
- value_momentum: float32 [2048, 512], P('fsdp', 'replica'), may hold values from -0.09375 to 0.09375
Outputs:
- projected: bfloat16 [65536, 3072], P(('replica', 'fsdp'))
- updated_outer_query: float32 [2048, 2048], P('fsdp')
- updated_outer_key: float32 [2048, 512], P('fsdp')
- new_outer_v: float32 [2048, 512], P('fsdp')
- new_moment_q: float32 [2048, 2048], P('fsdp', 'replica')
- new_moment_k: float32 [2048, 512], P('fsdp', 'replica')
- new_moment_v: float32 [2048, 512], P('fsdp', 'replica')
All inputs are finite; a program needn't handle non-finite values.
Results may differ from a plain program's by a relative error of at most 0.005.
Values may be sent and summed in bfloat16 or wider, within the bound.
A program may use at most 64 MiB of HBM per device.

v0:
```python
import jax
import jax.numpy as jnp
from jax import lax
from jax.sharding import PartitionSpec as P

LEARN_RATE = 0.7
MOMENTUM_BETA = 0.9


def per_device(
    tokens, inner_q, inner_k, inner_v, outer_q, outer_k, outer_v, moment_q, moment_k, value_momentum
):
    worker_count = lax.axis_size("replica")
    worker_index = lax.axis_index("replica")
    outers = (outer_q, outer_k, outer_v)
    moments = (moment_q, moment_k, value_momentum)
    differences = tuple(
        (
            outer - inner[0].astype(jnp.float32)
            for outer, inner in zip(outers, (inner_q, inner_k, inner_v))
        )
    )
    summed = lax.psum_scatter(differences, "replica", scatter_dimension=1, tiled=True)
    owned_outer = []
    owned_moment = []
    for total, outer, outer_momentum in zip(summed, outers, moments):
        width = outer_momentum.shape[1]
        pseudo = total / worker_count
        new_moment = MOMENTUM_BETA * outer_momentum + pseudo
        own_slice = lax.dynamic_slice_in_dim(outer, worker_index * width, width, 1)
        owned_outer.append(own_slice - LEARN_RATE * (pseudo + MOMENTUM_BETA * new_moment))
        owned_moment.append(new_moment)
    full_outer = lax.all_gather(tuple(owned_outer), "replica", axis=1, tiled=True)
    local_fresh = jnp.concatenate([weight.astype(jnp.bfloat16) for weight in full_outer], axis=1)
    fresh = lax.all_gather(local_fresh, "fsdp", axis=0, tiled=True)
    projected = jnp.dot(tokens, fresh, preferred_element_type=jnp.float32).astype(jnp.bfloat16)
    return (
        projected,
        full_outer[0],
        full_outer[1],
        full_outer[2],
        owned_moment[0],
        owned_moment[1],
        owned_moment[2],
    )


def solution(mesh):
    placed = (
        P(("replica", "fsdp"), None),
        P("replica", "fsdp", None),
        P("replica", "fsdp", None),
        P("replica", "fsdp", None),
        P("fsdp", None),
        P("fsdp", None),
        P("fsdp", None),
        P("fsdp", "replica"),
        P("fsdp", "replica"),
        P("fsdp", "replica"),
    )
    return jax.shard_map(
        per_device,
        mesh=mesh,
        in_specs=placed,
        out_specs=(
            P(("replica", "fsdp"), None),
            P("fsdp", None),
            P("fsdp", None),
            P("fsdp", None),
            P("fsdp", "replica"),
            P("fsdp", "replica"),
            P("fsdp", "replica"),
        ),
        check_vma=False,
    )
```

profile of v0, /device:TPU:16, one launch (start us, length us, event | category | flops | bytes accessed | tf_op | source)
XLA Modules:
  0.0 515.0 jit_solution(6536881610488813657)
XLA Ops:
  7.2 0.0 copy-start
  7.2 0.0 reduce-scatter.6.cloned.1.call-start
  7.2 1.6 convert_subtract_fusion.2
  8.8 0.0 reduce-scatter.6.cloned.1.call-update
  8.8 0.0 reduce-scatter.8.cloned.1.call-start
  8.9 1.5 convert_subtract_fusion.1
  10.3 0.0 reduce-scatter.8.cloned.1.call-update
  10.4 0.0 reduce-scatter.4.cloned.1.call-start
  10.4 1.7 convert_subtract_fusion
  12.1 0.0 reduce-scatter.4.cloned.1.call-update
  12.2 0.0 all-gather.2.cloned.1.call-start
  12.2 36.2 %reduce-scatter.6.cloned.1.call-done = f32[32,128]{1,0:T(8,128)} async-done(((f32[32,512]{1,0:T(8,128)}), f32[32,128]{1,0:T(8,128)}) %reduce-scatter.6.cloned.1.call-update) | async-done | bytes 16400 | tf_op jit(solution)/shard_map/reduce_scatter | solution.py:23
  48.4 1.4 multiply_subtract_fusion.2
  49.8 9.1 %all_gather.13 = f32[32,512]{1,0:T(8,128)S(1)} all-gather(f32[32,128]{1,0:T(8,128)S(1)} %get-tuple-element.16), channel_id=1, replica_groups=mesh['replica'=4,'fsdp'=64] {'replica'}, dimensions={1}, use_global_device_ids=true | all-gather | bytes 81920 | tf_op jit(solution)/shard_map/all_gather | solution.py:33
  58.9 23.6 %reduce-scatter.8.cloned.1.call-done = f32[32,128]{1,0:T(8,128)} async-done(((f32[32,512]{1,0:T(8,128)}), f32[32,128]{1,0:T(8,128)}) %reduce-scatter.8.cloned.1.call-update) | async-done | bytes 16400 | tf_op jit(solution)/shard_map/reduce_scatter | solution.py:23
  82.5 1.4 multiply_subtract_fusion.1
  83.9 9.1 %all_gather.14 = f32[32,512]{1,0:T(8,128)S(1)} all-gather(f32[32,128]{1,0:T(8,128)S(1)} %get-tuple-element.18), channel_id=1, replica_groups=mesh['replica'=4,'fsdp'=64] {'replica'}, dimensions={1}, use_global_device_ids=true | all-gather | bytes 81920 | tf_op jit(solution)/shard_map/all_gather | solution.py:33
  93.0 25.5 %reduce-scatter.4.cloned.1.call-done = f32[32,512]{1,0:T(8,128)} async-done(((f32[32,2048]{1,0:T(8,128)}), f32[32,512]{1,0:T(8,128)}) %reduce-scatter.4.cloned.1.call-update) | async-done | bytes 65552 | tf_op jit(solution)/shard_map/reduce_scatter | solution.py:23
  118.5 1.5 multiply_subtract_fusion
  120.1 9.7 %all_gather.12 = f32[32,2048]{1,0:T(8,128)S(1)} all-gather(f32[32,512]{1,0:T(8,128)S(1)} %get-tuple-element.14), channel_id=1, replica_groups=mesh['replica'=4,'fsdp'=64] {'replica'}, dimensions={1}, use_global_device_ids=true | all-gather | bytes 327680 | tf_op jit(solution)/shard_map/all_gather | solution.py:33
  129.8 0.7 pad_maximum_fusion
  130.5 0.0 all-gather.2.cloned.1.call-update
  130.5 365.9 %all-gather.2.cloned.1.call-done = bf16[2048,3072]{1,0:T(8,128)(2,1)} async-done(((bf16[32,3072]{1,0:T(8,128)(2,1)}), bf16[2048,3072]{1,0:T(8,128)(2,1)}) %all-gather.2.cloned.1.call-update) | async-done | bytes 12582928 | tf_op jit(solution)/shard_map/all_gather | solution.py:35
  496.4 0.0 copy-done
  496.4 8.3 %fusion = bf16[256,3072]{0,1:T(8,128)(2,1)S(1)} fusion(bf16[2048,3072]{1,0:T(8,128)(2,1)} %all-gather.2.cloned.1.call-done, bf16[256,2048]{1,0:T(8,128)(2,1)S(1)} %copy-done), kind=kOutput, calls=%fused_computation.1 | convolution fusion | flops 3222011904 | bytes 15204352 | tf_op jit(solution)/shard_map/dot_general | solution.py:36
  504.7 1.7 copy.17
  506.5 0.7 copy.21
  507.2 0.6 copy.22
  507.8 0.6 copy.23
  (3 shorter events, 0.0 us)
Async XLA Ops:
  7.2 489.2 %copy-start = (bf16[256,2048]{1,0:T(8,128)(2,1)S(1)}, bf16[256,2048]{1,0:T(8,128)(2,1)}, u32[]{:S(2)}) copy-start(bf16[256,2048]{1,0:T(8,128)(2,1)} %param.10) | copy-start | bytes 3145732
  7.2 41.2 %reduce-scatter.6.cloned.1.call-start = ((), (), s32[]{:S(2)}) async-start(), calls=%async_computation.4 | async-start | bytes 81920 | tf_op jit(solution)/shard_map/reduce_scatter | solution.py:23
  8.8 73.7 %reduce-scatter.8.cloned.1.call-start = ((), (), s32[]{:S(2)}) async-start(), calls=%async_computation.5 | async-start | bytes 81920 | tf_op jit(solution)/shard_map/reduce_scatter | solution.py:23
  10.4 108.2 %reduce-scatter.4.cloned.1.call-start = ((), (), s32[]{:S(2)}) async-start(), calls=%async_computation.3 | async-start | bytes 327680 | tf_op jit(solution)/shard_map/reduce_scatter | solution.py:23
  12.2 484.3 %all-gather.2.cloned.1.call-start = ((), (), s32[]{:S(2)}) async-start(), calls=%async_computation.6 | async-start | bytes 12779520 | tf_op jit(solution)/shard_map/all_gather | solution.py:35
Sparse Core Ops, SparseCore 0:
  11.2 37.1 reduce-scatter.5
  51.6 30.8 reduce-scatter.7
  85.8 32.7 reduce-scatter.3
  130.6 365.7 all-gather.1
where the time goes:
time: 515 us
  waiting for transfers between devices  451 us (88%)
  blocking collectives  27.9 us (5%)
  between operations  13.8 us (3%)
  other arithmetic  9.75 us (2%)
  matrix products  8.3 us (2%)
    all_gather x1, waiting for transfers between devices, per_device(): fresh = lax.all_gather(local_fresh, 'fsdp', axis=0, tiled=True)  366 us
    reduce_scatter x3, waiting for transfers between devices, per_device(): lax.psum_scatter(differences, 'replica', scatter_dimension=1, tiled=True)  85.3 us
    all_gather x3, blocking collectives, per_device(): lax.all_gather(tuple(owned_outer), 'replica', axis=1, tiled=True)  27.9 us
  transfers between devices with their start and end apart: 4, of which 4 were waited for; matrix products, arithmetic and copies ran while one was open for 1% of the time, Pallas kernels for 0%

commit v1 on v0

v1 whole, which is shorter than its diff:
```python
import functools
import heapq

import jax
import jax.numpy as jnp
from jax import lax
from jax.experimental import pallas as pl
from jax.experimental.pallas import tpu as pltpu
from jax.sharding import PartitionSpec as P

LEARN_RATE = 0.7
MOMENTUM_BETA = 0.9
MESH = pl.DeviceIdType.MESH

NX, NY, NZ = 4, 4, 8
SIZE = {"x": NX, "y": NY, "z": NZ}
ROWS = 32
WIDTH = 256
ORDERS = (("x", "y", "z"), ("z", "y", "x"), ("z", "x", "y"))


def subs_of(colour, phase):
    if phase == 0:
        return (None,)
    if colour == 0:
        return (None,) if phase == 1 else tuple((d, None) for d in (0, 3, 1, 2))
    if phase == 1:
        return (0, 1)
    return tuple((d, k) for d in (0, 3, 1, 2) for k in (0, 1))


def reach(colour, phase, sub):
    n = SIZE[ORDERS[colour][phase]]
    subs = subs_of(colour, phase)
    odd = subs.index(sub) % 2 if len(subs) > 1 else (colour + phase) % 2
    return (n // 2, n - 1 - n // 2) if odd == 0 else (n - 1 - n // 2, n // 2)


def all_messages():
    out = []
    for colour in range(3):
        for phase in range(3):
            for sub in subs_of(colour, phase):
                plus, minus = reach(colour, phase, sub)
                out += [(colour, phase, sub, 1, s) for s in range(1, plus + 1)]
                out += [(colour, phase, sub, -1, s) for s in range(1, minus + 1)]
    return out


MESSAGES = all_messages()
INDEX = {m: i for i, m in enumerate(MESSAGES)}


class Flow:
    def __init__(self, send):
        self.send = send
        self.first = [0, 0, 0]

    def begin(self, colour, phase, sub):
        plus, minus = reach(colour, phase, sub)
        for direction, hops in ((1, plus), (-1, minus)):
            if hops >= 1:
                self.send((colour, phase, sub, direction, 1))

    def received(self, message):
        colour, phase, sub, direction, step = message
        plus, minus = reach(colour, phase, sub)
        if step < (plus if direction == 1 else minus):
            self.send((colour, phase, sub, direction, step + 1))
        if phase == 0:
            self.first[colour] += 1
            if self.first[colour] == SIZE[ORDERS[colour][0]] - 1:
                for k in subs_of(colour, 1):
                    self.begin(colour, 1, k)
                for k in subs_of(colour, 1):
                    self.begin(colour, 2, (0, k))
        elif phase == 1:
            offset = (-direction * step) % SIZE[ORDERS[colour][1]]
            self.begin(colour, 2, (offset, sub))


def plan(starts):
    free, heap = {}, []
    now = [0.0]

    def send(message):
        colour, phase, sub, direction, step = message
        size = 16384 if phase == 0 else 65536
        link = (ORDERS[colour][phase], direction)
        begin = max(now[0], free.get(link, 0.0))
        free[link] = begin + size / 46e3
        heapq.heappush(heap, (free[link] + 1.7, INDEX[message]))

    flow = Flow(send)
    order = []
    for colour, start in enumerate(starts):
        heapq.heappush(heap, (start, -1 - colour))
    while heap:
        now[0], which = heapq.heappop(heap)
        order.append(which)
        if which < 0:
            flow.begin(-1 - which, 0, None)
        else:
            flow.received(MESSAGES[which])
    return order, now[0]


PLAN, MODEL_TIME = plan((3.0, 0.0, 1.5))


def kernel(
    tok, iq, ik, iv, oq, ok, ov, mq, mk, mv,
    proj, uq, uk, uv, nq, nk, nv,
    buf, tok2, ri, fr, pout,
    rep_sem, ring_sem, tok_sem, fr_sem, out_sem, rep_send, ring_send, fr_send, out_send, tok_send, tok_local,
):
    r, f = lax.axis_index("replica"), lax.axis_index("fsdp")
    core, zh = r % 2, r // 2
    zl, x, y = f // 16, (f // 4) % 4, f % 4
    z = zh * 4 + zl
    at = {"x": x, "y": y, "z": z}

    def dev(xx, yy, zz):
        return {"replica": (zz // 4) * 2 + core, "fsdp": ((zz % 4) * 4 + xx) * 4 + yy}

    def neighbour(axis, direction):
        moved = dict(at)
        moved[axis] = (at[axis] + direction + SIZE[axis]) % SIZE[axis]
        return dev(moved["x"], moved["y"], moved["z"])

    peer_index = (zh * 2 + (1 - core), (1 - zh) * 2 + core, (1 - zh) * 2 + (1 - core))
    peers = tuple({"replica": p, "fsdp": f} for p in peer_index)
    neighbours = {(a, d): neighbour(a, d) for a in ("x", "y", "z") for d in (1, -1)}

    barrier = pltpu.get_barrier_semaphore()
    for target in peers + tuple(neighbours.values()):
        pl.semaphore_signal(barrier, inc=1, device_id=target, device_id_type=MESH)
    own_tokens = pltpu.make_async_copy(tok, tok2.at[0], tok_local)
    own_tokens.start()
    pl.semaphore_wait(barrier, 9)

    def remote(src, dst, send_sem, recv_sem, target):
        return pltpu.make_async_remote_copy(
            src_ref=src, dst_ref=dst, send_sem=send_sem, recv_sem=recv_sem, device_id=target, device_id_type=MESH
        )

    def col(index, width, extra=0):
        return pl.ds(pl.multiple_of(index * width + extra, 128), WIDTH if width == 512 else 128)

    def replica_copies(colour, d):
        p = peer_index[d]
        if colour < 2:
            pairs = ((iq.at[:, col(p, 512, colour * WIDTH)], ri.at[d, colour]),)
        else:
            pairs = (
                (ik.at[:, col(p, 128)], ri.at[d, 2, :, 0:128]),
                (iv.at[:, col(p, 128)], ri.at[d, 2, :, 128:256]),
            )
        return [
            remote(src, dst, rep_send.at[d, colour + i], rep_sem.at[d, colour + i], peers[d])
            for i, (src, dst) in enumerate(pairs)
        ]

    copies = {}
    for colour in (1, 2, 0):
        for d in (1, 2, 0):
            copies[colour, d] = replica_copies(colour, d)
            for c in copies[colour, d]:
                c.start()
    swap = remote(tok, tok2.at[1], tok_send, tok_sem, peers[0])
    swap.start()

    def update(colour):
        for d in range(3):
            for c in copies[colour, d]:
                c.wait_recv()
        if colour < 2:
            outer = oq[:, col(r, 512, colour * WIDTH)]
            inner = iq[:, col(r, 512, colour * WIDTH)]
            moment = mq[:, colour * WIDTH:(colour + 1) * WIDTH]
        else:
            outer = jnp.concatenate([ok[:, col(r, 128)], ov[:, col(r, 128)]], axis=1)
            inner = jnp.concatenate([ik[:, col(r, 128)], iv[:, col(r, 128)]], axis=1)
            moment = jnp.concatenate([mk[...], mv[...]], axis=1)
        total = outer - inner.astype(jnp.float32)
        for d in range(3):
            total += outer - ri[d, colour].astype(jnp.float32)
        pseudo = total * 0.25
        new_moment = MOMENTUM_BETA * moment + pseudo
        new_outer = outer - LEARN_RATE * (pseudo + MOMENTUM_BETA * new_moment)
        buf[colour, z, x, y] = new_outer.astype(jnp.bfloat16)
        if colour < 2:
            nq[:, colour * WIDTH:(colour + 1) * WIDTH] = new_moment
        else:
            nk[...] = new_moment[:, :128]
            nv[...] = new_moment[:, 128:]

    def block(colour, phase, sub, offset):
        axis = ORDERS[colour][phase]
        pos = dict(at)
        if phase == 2:
            second = ORDERS[colour][1]
            pos[second] = (at[second] + sub[0]) % SIZE[second]
            sub = sub[1]
        pos[axis] = (at[axis] + offset + SIZE[axis]) % SIZE[axis]
        if phase == 0:
            return buf.at[colour, pos["z"], pos["x"], pos["y"]]
        if colour == 0:
            return buf.at[0, pos["z"], :, pos["y"]]
        return buf.at[colour, pl.ds(sub * 4, 4), pos["x"], pos["y"]]

    def ring_copy(message):
        colour, phase, sub, direction, step = message
        src = block(colour, phase, sub, -direction * (step - 1))
        return remote(src, src, ring_send, ring_sem.at[INDEX[message]], neighbours[ORDERS[colour][phase], direction])

    def wait_ring(message):
        colour, phase, sub, direction, step = message
        dst = block(colour, phase, sub, -direction * step)
        remote(dst, dst, ring_send, ring_sem.at[INDEX[message]], neighbours[ORDERS[colour][phase], direction]).wait_recv()

    flow = Flow(lambda message: ring_copy(message).start())
    partner_copies = []
    for which in PLAN:
        if which < 0:
            colour = -1 - which
            update(colour)
            flow.begin(colour, 0, None)
            c = remote(buf.at[colour, z, x, y], fr.at[0, colour], fr_send.at[0, colour], fr_sem.at[0, colour], peers[0])
            c.start()
            partner_copies.append(c)
        else:
            wait_ring(MESSAGES[which])
            flow.received(MESSAGES[which])

    z4 = (z + 4) % 8
    for colour in range(3):
        c = remote(buf.at[colour, z4, x, y], fr.at[1, colour], fr_send.at[1, colour], fr_sem.at[1, colour], peers[0])
        c.start()
        partner_copies.append(c)

    own_tokens.wait()
    swap.wait()

    out_copies = []

    def send_out(i):
        colour, h = i // 2, i % 2
        rr = 2 * h + core
        if colour < 2:
            pairs = ((pout.at[i], proj.at[:, col(rr, 512, colour * WIDTH)]),)
        else:
            pairs = (
                (pout.at[i, :, 0:128], proj.at[:, col(rr, 128, 2048)]),
                (pout.at[i, :, 128:256], proj.at[:, col(rr, 128, 2560)]),
            )
        for j, (src, dst) in enumerate(pairs):
            c = remote(src, dst, out_send.at[i, j], out_sem.at[i, j], peers[0])
            c.start()
            out_copies.append(c)

    for i in range(6):
        colour, h = i // 2, i % 2
        rr = 2 * h + core
        w = buf[colour, h * 4:(h + 1) * 4].reshape(2048, WIDTH)
        acc = jnp.dot(tok2[...].reshape(512, 2048), w, preferred_element_type=jnp.float32).astype(jnp.bfloat16)
        pout[i] = acc[256:]
        if colour < 2:
            proj[:, col(rr, 512, colour * WIDTH)] = acc[:256]
        else:
            proj[:, col(rr, 128, 2048)] = acc[:256, :128]
            proj[:, col(rr, 128, 2560)] = acc[:256, 128:]
        if i >= 1:
            send_out(i - 1)
    send_out(5)

    for c in partner_copies:
        c.wait()
    for source, owner in (
        (lambda c: buf[c, z, x, y], r),
        (lambda c: buf[c, z4, x, y], peer_index[1]),
        (lambda c: fr[0, c], peer_index[0]),
        (lambda c: fr[1, c], peer_index[2]),
    ):
        for colour in range(2):
            uq[:, col(owner, 512, colour * WIDTH)] = source(colour).astype(jnp.float32)
        both = source(2).astype(jnp.float32)
        uk[:, col(owner, 128)] = both[:, :128]
        uv[:, col(owner, 128)] = both[:, 128:]

    for c in out_copies:
        c.wait()
    for colour in range(3):
        for d in range(3):
            for c in copies[colour, d]:
                c.wait_send()
    for colour in range(3):
        done = buf.at[colour].reshape(128, ROWS, WIDTH).at[pl.ds(0, 127)]
        pltpu.make_async_copy(done, done, ring_send).wait()


def per_device(
    tokens, inner_q, inner_k, inner_v, outer_q, outer_k, outer_v, moment_q, moment_k, value_momentum
):
    f32, bf16 = jnp.float32, jnp.bfloat16
    vmem = pl.BlockSpec(memory_space=pltpu.VMEM)
    out = pl.pallas_call(
        kernel,
        out_shape=(
            jax.ShapeDtypeStruct((256, 3072), bf16),
            jax.ShapeDtypeStruct((ROWS, 2048), f32),
            jax.ShapeDtypeStruct((ROWS, 512), f32),
            jax.ShapeDtypeStruct((ROWS, 512), f32),
            jax.ShapeDtypeStruct((ROWS, 512), f32),
            jax.ShapeDtypeStruct((ROWS, 128), f32),
            jax.ShapeDtypeStruct((ROWS, 128), f32),
        ),
        in_specs=[pl.BlockSpec(memory_space=pl.ANY)] + [vmem] * 9,
        out_specs=(vmem,) * 7,
        scratch_shapes=[
            pltpu.VMEM((3, NZ, NX, NY, ROWS, WIDTH), bf16),
            pltpu.VMEM((2, 256, 2048), bf16),
            pltpu.VMEM((3, 3, ROWS, WIDTH), bf16),
            pltpu.VMEM((2, 3, ROWS, WIDTH), bf16),
            pltpu.VMEM((6, 256, WIDTH), bf16),
            pltpu.SemaphoreType.DMA((3, 4)),
            pltpu.SemaphoreType.DMA((len(MESSAGES),)),
            pltpu.SemaphoreType.DMA,
            pltpu.SemaphoreType.DMA((2, 3)),
            pltpu.SemaphoreType.DMA((6, 2)),
            pltpu.SemaphoreType.DMA((3, 4)),
            pltpu.SemaphoreType.DMA,
            pltpu.SemaphoreType.DMA((2, 3)),
            pltpu.SemaphoreType.DMA((6, 2)),
            pltpu.SemaphoreType.DMA,
            pltpu.SemaphoreType.DMA,
        ],
        compiler_params=pltpu.CompilerParams(
            collective_id=0, has_side_effects=True, vmem_limit_bytes=48 * 1024 * 1024
        ),
        name="outer_step_gather_project",
    )(tokens, inner_q[0], inner_k[0], inner_v[0], outer_q, outer_k, outer_v, moment_q, moment_k, value_momentum)
    return tuple(out)


def solution(mesh):
    placed = (
        P(("replica", "fsdp"), None),
        P("replica", "fsdp", None),
        P("replica", "fsdp", None),
        P("replica", "fsdp", None),
        P("fsdp", None),
        P("fsdp", None),
        P("fsdp", None),
        P("fsdp", "replica"),
        P("fsdp", "replica"),
        P("fsdp", "replica"),
    )
    return jax.shard_map(
        per_device,
        mesh=mesh,
        in_specs=placed,
        out_specs=(
            P(("replica", "fsdp"), None),
            P("fsdp", None),
            P("fsdp", None),
            P("fsdp", None),
            P("fsdp", "replica"),
            P("fsdp", "replica"),
            P("fsdp", "replica"),
        ),
        check_vma=False,
    )
```

time: 515 us -> 76.4 us (0.15)
  the two profiles are of different devices: /device:TPU:16 before, /device:TPU:1 now
where the time goes in v1:
time: 76.4 us; the launch traced here: 75.9 us
  Pallas kernels  61.7 us (81%)
  local copies, waits for them, and re-layouts  13.5 us (18%)
    pallas_call x1, Pallas kernels, per_device(): pl.pallas_call(kernel, out_shape=(jax.ShapeDtypeStruct((256, 3072), bf16)...  61.7 us
    unnamed x27, local copies, waits for them, and re-layouts  13.5 us

profile of v1, /device:TPU:1, one launch (start us, length us, event | category | flops | bytes accessed | tf_op | source)
XLA Modules:
  0.0 75.9 jit_solution(11998027118084455071)
XLA Ops:
  0.6 0.0 copy-start
  0.6 1.2 %copy-done = bf16[256,2048]{1,0:T(8,128)(2,1)S(1)} copy-done((bf16[256,2048]{1,0:T(8,128)(2,1)S(1)}, bf16[256,2048]{1,0:T(8,128)(2,1)}, u32[]{:S(2)}) %copy-start) | copy-done | bytes 1048600
  1.9 0.0 copy-start.1
  1.9 0.9 %copy-done.1 = f32[32,2048]{1,0:T(8,128)S(1)} copy-done((f32[32,2048]{1,0:T(8,128)S(1)}, f32[32,2048]{1,0:T(8,128)}, u32[]{:S(2)}) %copy-start.1) | copy-done | bytes 262168
  2.8 0.0 copy-start.2
  2.8 0.9 %copy-done.2 = bf16[1,32,2048]{2,1,0:T(8,128)(2,1)S(1)} copy-done((bf16[1,32,2048]{2,1,0:T(8,128)(2,1)S(1)}, bf16[1,32,2048]{2,1,0:T(8,128)(2,1)}, u32[]{:S(2)}) %copy-start.2) | copy-done | bytes 131096
  3.7 0.0 copy-start.3
  3.7 0.8 %copy-done.3 = f32[32,512]{1,0:T(8,128)S(1)} copy-done((f32[32,512]{1,0:T(8,128)S(1)}, f32[32,512]{1,0:T(8,128)}, u32[]{:S(2)}) %copy-start.3) | copy-done | bytes 65560
  4.6 0.0 copy-start.4
  4.6 0.8 %copy-done.4 = f32[32,512]{1,0:T(8,128)S(1)} copy-done((f32[32,512]{1,0:T(8,128)S(1)}, f32[32,512]{1,0:T(8,128)}, u32[]{:S(2)}) %copy-start.4) | copy-done | bytes 65560
  5.4 0.0 copy-start.5
  5.4 0.8 %copy-done.5 = f32[32,512]{1,0:T(8,128)S(1)} copy-done((f32[32,512]{1,0:T(8,128)S(1)}, f32[32,512]{1,0:T(8,128)}, u32[]{:S(2)}) %copy-start.5) | copy-done | bytes 65560
  6.2 0.0 copy-start.6
  6.2 0.8 copy-done.6
  7.0 0.0 copy-start.7
  7.0 0.8 copy-done.7
  7.8 0.0 copy-start.8
  7.8 0.7 copy-done.8
  8.5 0.0 copy-start.9
  8.5 0.7 copy-done.9
  9.2 61.7 %outer_step_gather_project.1 = (bf16[256,3072]{1,0:T(8,128)(2,1)S(1)}, f32[32,2048]{1,0:T(8,128)S(1)}, f32[32,512]{1,0:T(8,128)S(1)}, f32[32,512]{1,0:T(8,128)S(...) custom-call(bf16[256,2048]{1,0:T(8,128)(2,1)S(1)} %copy-done, ...), custom_call_target="tpu_custom_call" | custom-call | tf_op jit(solution)/shard_map/outer_step_gather_project/pallas_call | solution.py:307
  70.9 1.1 %copy.24 = bf16[256,3072]{1,0:T(8,128)(2,1)} copy(bf16[256,3072]{1,0:T(8,128)(2,1)S(1)} %get-tuple-element.14) | data formatting | bytes 3145728
  72.1 0.7 copy.25
  72.8 0.6 copy.26
  73.4 0.6 copy.27
  74.0 0.6 copy.28
  74.7 0.6 copy.29
  75.3 0.6 copy.30
Async XLA Ops:
  0.6 1.2 %copy-start = (bf16[256,2048]{1,0:T(8,128)(2,1)S(1)}, bf16[256,2048]{1,0:T(8,128)(2,1)}, u32[]{:S(2)}) copy-start(bf16[256,2048]{1,0:T(8,128)(2,1)} %tok.1) | copy-start | bytes 3145732
  1.9 0.9 %copy-start.1 = (f32[32,2048]{1,0:T(8,128)S(1)}, f32[32,2048]{1,0:T(8,128)}, u32[]{:S(2)}) copy-start(f32[32,2048]{1,0:T(8,128)} %oq.1) | copy-start | bytes 786436
  2.8 0.9 %copy-start.2 = (bf16[1,32,2048]{2,1,0:T(8,128)(2,1)S(1)}, bf16[1,32,2048]{2,1,0:T(8,128)(2,1)}, u32[]{:S(2)}) copy-start(bf16[1,32,2048]{2,1,0:T(8,128)(2,1)} %param.11) | copy-start | bytes 393220
  3.7 0.8 %copy-start.3 = (f32[32,512]{1,0:T(8,128)S(1)}, f32[32,512]{1,0:T(8,128)}, u32[]{:S(2)}) copy-start(f32[32,512]{1,0:T(8,128)} %ok.1) | copy-start | bytes 196612
  4.6 0.8 %copy-start.4 = (f32[32,512]{1,0:T(8,128)S(1)}, f32[32,512]{1,0:T(8,128)}, u32[]{:S(2)}) copy-start(f32[32,512]{1,0:T(8,128)} %ov.1) | copy-start | bytes 196612
  5.4 0.8 %copy-start.5 = (f32[32,512]{1,0:T(8,128)S(1)}, f32[32,512]{1,0:T(8,128)}, u32[]{:S(2)}) copy-start(f32[32,512]{1,0:T(8,128)} %mq.1) | copy-start | bytes 196612
  6.2 0.8 copy-start.6
  7.0 0.8 copy-start.7
  7.8 0.7 copy-start.8
  8.5 0.7 copy-start.9

commit v2 on v1

--- a/solution.py
+++ b/solution.py
@@ -109,8 +109,9 @@
 
 
 def kernel(
-    tok, iq, ik, iv, oq, ok, ov, mq, mk, mv,
+    tok, iq_hbm, ik_hbm, iv_hbm, oq_hbm, ok_hbm, ov_hbm, mq_hbm, mk_hbm, mv_hbm,
     proj, uq, uk, uv, nq, nk, nv,
+    iq, ik, iv, oq, ok, ov, mq, mk, mv, in_sem,
     buf, tok2, ri, fr, pout,
     rep_sem, ring_sem, tok_sem, fr_sem, out_sem, rep_send, ring_send, fr_send, out_send, tok_send, tok_local,
 ):
@@ -135,8 +136,21 @@
     barrier = pltpu.get_barrier_semaphore()
     for target in peers + tuple(neighbours.values()):
         pl.semaphore_signal(barrier, inc=1, device_id=target, device_id_type=MESH)
+    fetches = [
+        pltpu.make_async_copy(src, dst, in_sem.at[i])
+        for i, (src, dst) in enumerate(
+            zip(
+                (iq_hbm, ik_hbm, iv_hbm, oq_hbm, ok_hbm, ov_hbm, mq_hbm, mk_hbm, mv_hbm),
+                (iq, ik, iv, oq, ok, ov, mq, mk, mv),
+            )
+        )
+    ]
+    for c in fetches:
+        c.start()
     own_tokens = pltpu.make_async_copy(tok, tok2.at[0], tok_local)
     own_tokens.start()
+    for c in fetches:
+        c.wait()
     pl.semaphore_wait(barrier, 9)
 
     def remote(src, dst, send_sem, recv_sem, target):
@@ -297,6 +311,27 @@
     for colour in range(3):
         done = buf.at[colour].reshape(128, ROWS, WIDTH).at[pl.ds(0, 127)]
         pltpu.make_async_copy(done, done, ring_send).wait()
+
+
+def write_kernel(*refs):
+    sources, targets, sem = refs[:7], refs[7:14], refs[14]
+    copies = [pltpu.make_async_copy(src, dst, sem.at[i]) for i, (src, dst) in enumerate(zip(sources, targets))]
+    for c in copies:
+        c.start()
+    for c in copies:
+        c.wait()
+
+
+def write_out(results):
+    return pl.pallas_call(
+        write_kernel,
+        out_shape=tuple(jax.ShapeDtypeStruct(a.shape, a.dtype) for a in results),
+        in_specs=[pl.BlockSpec(memory_space=pltpu.VMEM)] * 7,
+        out_specs=(pl.BlockSpec(memory_space=pltpu.HBM),) * 7,
+        scratch_shapes=[pltpu.SemaphoreType.DMA((7,))],
+        compiler_params=pltpu.CompilerParams(vmem_limit_bytes=16 * 1024 * 1024),
+        name="write_results",
+    )(*results)
 
 
 def per_device(
@@ -315,9 +350,19 @@
             jax.ShapeDtypeStruct((ROWS, 128), f32),
             jax.ShapeDtypeStruct((ROWS, 128), f32),
         ),
-        in_specs=[pl.BlockSpec(memory_space=pl.ANY)] + [vmem] * 9,
+        in_specs=[pl.BlockSpec(memory_space=pltpu.HBM)] * 10,
         out_specs=(vmem,) * 7,
         scratch_shapes=[
+            pltpu.VMEM((ROWS, 2048), bf16),
+            pltpu.VMEM((ROWS, 512), bf16),
+            pltpu.VMEM((ROWS, 512), bf16),
+            pltpu.VMEM((ROWS, 2048), f32),
+            pltpu.VMEM((ROWS, 512), f32),
+            pltpu.VMEM((ROWS, 512), f32),
+            pltpu.VMEM((ROWS, 512), f32),
+            pltpu.VMEM((ROWS, 128), f32),
+            pltpu.VMEM((ROWS, 128), f32),
+            pltpu.SemaphoreType.DMA((9,)),
             pltpu.VMEM((3, NZ, NX, NY, ROWS, WIDTH), bf16),
             pltpu.VMEM((2, 256, 2048), bf16),
             pltpu.VMEM((3, 3, ROWS, WIDTH), bf16),
@@ -336,11 +381,16 @@
             pltpu.SemaphoreType.DMA,
         ],
         compiler_params=pltpu.CompilerParams(
-            collective_id=0, has_side_effects=True, vmem_limit_bytes=48 * 1024 * 1024
+            collective_id=0, has_side_effects=True, vmem_limit_bytes=32 * 1024 * 1024
         ),
         name="outer_step_gather_project",
-    )(tokens, inner_q[0], inner_k[0], inner_v[0], outer_q, outer_k, outer_v, moment_q, moment_k, value_momentum)
-    return tuple(out)
+    )(*(
+        pltpu.with_memory_space_constraint(a, pltpu.HBM)
+        for a in (
+            tokens, inner_q[0], inner_k[0], inner_v[0], outer_q, outer_k, outer_v, moment_q, moment_k, value_momentum
+        )
+    ))
+    return tuple(write_out(out))
 
 
 def solution(mesh):

time: 76.4 us -> 64.1 us (0.84)
  local copies, waits for them, and re-layouts: 13.5 us -> 0 us
  Pallas kernels: 61.7 us -> 63.3 us
    unnamed x27 -> x0, local copies, waits for them, and re-layouts: 13.5 us -> none
    pallas_call x0 -> x1, Pallas kernels: none -> 1.35 us  [write_out(): pl.pallas_call(write_kernel, out_shape=tuple((jax.ShapeDtypeStruct(a.shap...]
where the time goes in v2:
time: 64.1 us; the launch traced here: 64 us
  Pallas kernels  63.3 us (99%)
    pallas_call x1, Pallas kernels, per_device(): pl.pallas_call(kernel, out_shape=(jax.ShapeDtypeStruct((256, 3072), bf16)...  62 us
    pallas_call x1, Pallas kernels, write_out(): pl.pallas_call(write_kernel, out_shape=tuple((jax.ShapeDtypeStruct(a.shap...  1.35 us

profile of v2, /device:TPU:1, one launch (start us, length us, event | category | flops | bytes accessed | tf_op | source)
XLA Modules:
  0.0 64.0 jit_solution(6859552250758136872)
XLA Ops:
  0.6 62.0 %outer_step_gather_project.1 = (bf16[256,3072]{1,0:T(8,128)(2,1)S(1)}, f32[32,2048]{1,0:T(8,128)S(1)}, f32[32,512]{1,0:T(8,128)S(1)}, f32[32,512]{1,0:T(8,128)S(...) custom-call(bf16[256,2048]{1,0:T(8,128)(2,1)} %tok.1, bf16[32,2048]{1,0:T(8,128)(2,1)} %bitcast.3, ...), custom_call_target="tpu_custom_call" | custom-call | tf_op jit(solution)/shard_map/outer_step_gather_project/pallas_call | solution.py:342
  62.6 1.3 %write_results.1 = (bf16[256,3072]{1,0:T(8,128)(2,1)}, f32[32,2048]{1,0:T(8,128)}, f32[32,512]{1,0:T(8,128)}, f32[32,512]{1,0:T(8,128)}, f32[32,512]{1,0:T(8,128...) custom-call(bf16[256,3072]{1,0:T(8,128)(2,1)S(1)} %get-tuple-element.14.refs_0_, f32[32,2048]{1,0:T(8,128)S(1)} %get-tuple-element.15.refs_1_, ...), custom_call_target="tpu_custom_call" | custom-call | tf_op jit(solution)/shard_map/write_results/pallas_call | solution.py:326

commit v3 on v2

--- a/solution.py
+++ b/solution.py
@@ -52,9 +52,28 @@
 
 
 class Flow:
-    def __init__(self, send):
-        self.send = send
+    def __init__(self, send, ready):
+        self.send, self.ready = send, ready
         self.first = [0, 0, 0]
+        self.missing = {(0, o): 4 if o else 6 for o in range(8)}
+        self.missing.update({(1, k): 22 for k in (0, 1)})
+        self.missing.update({(2, d, k): 4 if d else 10 for d in range(4) for k in (0, 1)})
+
+    def count(self, message):
+        colour, phase, sub, direction, step = message
+        offset = (-direction * step) % SIZE[ORDERS[colour][phase]]
+        if colour == 0:
+            pieces = ((0, offset if phase == 2 else 0),)
+        elif colour == 1:
+            pieces = ((1, 0), (1, 1)) if phase == 0 else ((1, sub if phase == 1 else sub[1]),)
+        elif phase == 0:
+            pieces = ((2, 0, 0), (2, 0, 1))
+        else:
+            pieces = ((2, offset, sub),) if phase == 1 else ((2,) + sub,)
+        for piece in pieces:
+            self.missing[piece] -= 1
+            if self.missing[piece] == 0:
+                self.ready(piece)
 
     def begin(self, colour, phase, sub):
         plus, minus = reach(colour, phase, sub)
@@ -77,6 +96,7 @@
         elif phase == 1:
             offset = (-direction * step) % SIZE[ORDERS[colour][1]]
             self.begin(colour, 2, (offset, sub))
+        self.count(message)
 
 
 def plan(starts):
@@ -91,12 +111,19 @@
         free[link] = begin + size / 46e3
         heapq.heappush(heap, (free[link] + 1.7, INDEX[message]))
 
-    flow = Flow(send)
+    pending = []
+    flow = Flow(send, pending.append)
     order = []
     for colour, start in enumerate(starts):
         heapq.heappush(heap, (start, -1 - colour))
-    while heap:
-        now[0], which = heapq.heappop(heap)
+    while heap or pending:
+        if pending and not (heap and heap[0][0] <= now[0]):
+            piece = pending.pop(0)
+            order.append(piece)
+            now[0] += 0.9 if piece[0] == 1 else 0.3
+            continue
+        arrival, which = heapq.heappop(heap)
+        now[0] = max(now[0], arrival)
         order.append(which)
         if which < 0:
             flow.begin(-1 - which, 0, None)
@@ -112,7 +139,7 @@
     tok, iq_hbm, ik_hbm, iv_hbm, oq_hbm, ok_hbm, ov_hbm, mq_hbm, mk_hbm, mv_hbm,
     proj, uq, uk, uv, nq, nk, nv,
     iq, ik, iv, oq, ok, ov, mq, mk, mv, in_sem,
-    buf, tok2, ri, fr, pout,
+    buf, tok2, ri, fr, pout, acc,
     rep_sem, ring_sem, tok_sem, fr_sem, out_sem, rep_send, ring_send, fr_send, out_send, tok_send, tok_local,
 ):
     r, f = lax.axis_index("replica"), lax.axis_index("fsdp")
@@ -233,29 +260,6 @@
         dst = block(colour, phase, sub, -direction * step)
         remote(dst, dst, ring_send, ring_sem.at[INDEX[message]], neighbours[ORDERS[colour][phase], direction]).wait_recv()
 
-    flow = Flow(lambda message: ring_copy(message).start())
-    partner_copies = []
-    for which in PLAN:
-        if which < 0:
-            colour = -1 - which
-            update(colour)
-            flow.begin(colour, 0, None)
-            c = remote(buf.at[colour, z, x, y], fr.at[0, colour], fr_send.at[0, colour], fr_sem.at[0, colour], peers[0])
-            c.start()
-            partner_copies.append(c)
-        else:
-            wait_ring(MESSAGES[which])
-            flow.received(MESSAGES[which])
-
-    z4 = (z + 4) % 8
-    for colour in range(3):
-        c = remote(buf.at[colour, z4, x, y], fr.at[1, colour], fr_send.at[1, colour], fr_sem.at[1, colour], peers[0])
-        c.start()
-        partner_copies.append(c)
-
-    own_tokens.wait()
-    swap.wait()
-
     out_copies = []
 
     def send_out(i):
@@ -273,20 +277,77 @@
             c.start()
             out_copies.append(c)
 
-    for i in range(6):
+    def finish(i, total):
         colour, h = i // 2, i % 2
         rr = 2 * h + core
-        w = buf[colour, h * 4:(h + 1) * 4].reshape(2048, WIDTH)
-        acc = jnp.dot(tok2[...].reshape(512, 2048), w, preferred_element_type=jnp.float32).astype(jnp.bfloat16)
-        pout[i] = acc[256:]
+        done = total.astype(jnp.bfloat16)
+        pout[i] = done[256:]
         if colour < 2:
-            proj[:, col(rr, 512, colour * WIDTH)] = acc[:256]
-        else:
-            proj[:, col(rr, 128, 2048)] = acc[:256, :128]
-            proj[:, col(rr, 128, 2560)] = acc[:256, 128:]
-        if i >= 1:
-            send_out(i - 1)
-    send_out(5)
+            proj[:, col(rr, 512, colour * WIDTH)] = done[:256]
+        else:
+            proj[:, col(rr, 128, 2048)] = done[:256, :128]
+            proj[:, col(rr, 128, 2560)] = done[:256, 128:]
+        send_out(i)
+
+    def product(a, w):
+        return jnp.dot(a, w, preferred_element_type=jnp.float32)
+
+    done_pieces = []
+
+    def multiply(piece):
+        if not done_pieces:
+            own_tokens.wait()
+            swap.wait()
+        done_pieces.append(piece)
+        if piece[0] == 0:
+            plane = (z + piece[1]) % 8
+            columns = pl.ds(pl.multiple_of((plane % 4) * 512, 512), 512)
+            part = product(tok2[:, :, columns].reshape(512, 512), buf[0, plane].reshape(512, WIDTH))
+            acc[plane // 4] += part
+            if sum(p[0] == 0 for p in done_pieces) == 8:
+                finish(0, acc[0])
+                finish(1, acc[1])
+        elif piece[0] == 1:
+            k = piece[1]
+            w = buf[1, k * 4:(k + 1) * 4].reshape(2048, WIDTH)
+            finish(2 + k, product(tok2[...].reshape(512, 2048), w))
+        else:
+            _, d, k = piece
+            xx = (x + d) % 4
+            a = jnp.concatenate(
+                [tok2[:, :, pl.ds(pl.multiple_of(q * 512 + xx * 128, 128), 128)] for q in range(4)], axis=2
+            )
+            part = product(a.reshape(512, 512), buf[2, k * 4:(k + 1) * 4, xx].reshape(512, WIDTH))
+            n = sum(p[0] == 2 and p[2] == k for p in done_pieces)
+            if n == 1:
+                acc[4 + k] = part
+            elif n < 4:
+                acc[4 + k] += part
+            else:
+                finish(4 + k, acc[4 + k] + part)
+
+    acc[0:2] = jnp.zeros((2, 512, WIDTH), jnp.float32)
+    flow = Flow(lambda message: ring_copy(message).start(), lambda piece: None)
+    partner_copies = []
+    for which in PLAN:
+        if isinstance(which, tuple):
+            multiply(which)
+        elif which < 0:
+            colour = -1 - which
+            update(colour)
+            flow.begin(colour, 0, None)
+            c = remote(buf.at[colour, z, x, y], fr.at[0, colour], fr_send.at[0, colour], fr_sem.at[0, colour], peers[0])
+            c.start()
+            partner_copies.append(c)
+        else:
+            wait_ring(MESSAGES[which])
+            flow.received(MESSAGES[which])
+
+    z4 = (z + 4) % 8
+    for colour in range(3):
+        c = remote(buf.at[colour, z4, x, y], fr.at[1, colour], fr_send.at[1, colour], fr_sem.at[1, colour], peers[0])
+        c.start()
+        partner_copies.append(c)
 
     for c in partner_copies:
         c.wait()
@@ -368,6 +429,7 @@
             pltpu.VMEM((3, 3, ROWS, WIDTH), bf16),
             pltpu.VMEM((2, 3, ROWS, WIDTH), bf16),
             pltpu.VMEM((6, 256, WIDTH), bf16),
+            pltpu.VMEM((6, 512, WIDTH), f32),
             pltpu.SemaphoreType.DMA((3, 4)),
             pltpu.SemaphoreType.DMA((len(MESSAGES),)),
             pltpu.SemaphoreType.DMA,

time: 64.1 us -> 61.6 us (0.961)
  Pallas kernels: 63.3 us -> 60.8 us
    pallas_call x1, Pallas kernels: 62 us -> 59.5 us  [per_device(): pl.pallas_call(kernel, out_shape=(jax.ShapeDtypeStruct((256, 3072), bf16)...]
where the time goes in v3:
time: 61.6 us; the launch traced here: 61.5 us
  Pallas kernels  60.8 us (99%)
  between operations  0.64 us (1%)
    pallas_call x1, Pallas kernels, per_device(): pl.pallas_call(kernel, out_shape=(jax.ShapeDtypeStruct((256, 3072), bf16)...  59.5 us
    pallas_call x1, Pallas kernels, write_out(): pl.pallas_call(write_kernel, out_shape=tuple((jax.ShapeDtypeStruct(a.shap...  1.35 us

profile of v3, /device:TPU:1, one launch (start us, length us, event | category | flops | bytes accessed | tf_op | source)
XLA Modules:
  0.0 61.5 jit_solution(11607257435894509237)
XLA Ops:
  0.6 59.5 %outer_step_gather_project.1 = (bf16[256,3072]{1,0:T(8,128)(2,1)S(1)}, f32[32,2048]{1,0:T(8,128)S(1)}, f32[32,512]{1,0:T(8,128)S(1)}, f32[32,512]{1,0:T(8,128)S(...) custom-call(bf16[256,2048]{1,0:T(8,128)(2,1)} %tok.1, bf16[32,2048]{1,0:T(8,128)(2,1)} %bitcast.3, ...), custom_call_target="tpu_custom_call" | custom-call | tf_op jit(solution)/shard_map/outer_step_gather_project/pallas_call | solution.py:403
  60.1 1.3 %write_results.1 = (bf16[256,3072]{1,0:T(8,128)(2,1)}, f32[32,2048]{1,0:T(8,128)}, f32[32,512]{1,0:T(8,128)}, f32[32,512]{1,0:T(8,128)}, f32[32,512]{1,0:T(8,128...) custom-call(bf16[256,3072]{1,0:T(8,128)(2,1)S(1)} %get-tuple-element.14.refs_0_, f32[32,2048]{1,0:T(8,128)S(1)} %get-tuple-element.15.refs_1_, ...), custom_call_target="tpu_custom_call" | custom-call | tf_op jit(solution)/shard_map/write_results/pallas_call | solution.py:387
